TPU v7x, 256 devices: a whole 4x4x8 slice. The times are simulated.
256 devices in a mesh: ctx: 16 (over z, core), exp: 16 (over x, y).
Axes of the slice: x: 4, y: 4, z: 8, core: 2. Of those that a mesh axis runs over, the one named last changes fastest.
Arguments:
- query_input: bfloat16 [2048, 8192], P('ctx', 'exp'), may hold values from -6 to 6
- key_input: bfloat16 [2048, 8192], P('ctx', 'exp'), may hold values from -6 to 6
- value_input: bfloat16 [2048, 8192], P('ctx', 'exp'), may hold values from -6 to 6
- gate_logits: float32 [2, 2048, 64], P(None, 'ctx', 'exp'), may hold values from -6 to 6
- comp_weight: float32 [2, 32, 64], P(None, None, 'exp'), may hold values from -6 to 6
- out_proj: bfloat16 [8192, 7168], P('exp', 'ctx'), may hold values from -0.0625 to 0.0625
- residual_in: bfloat16 [2048, 7168], P(('ctx', 'exp')), may hold values from -3 to 3
- ffn_gain: float32 [7168], replicated, may hold values from 0.25 to 1.75
- expert_ids: int32 [2048, 2], P(('ctx', 'exp')), may hold values from 0 to 15, all different within a row; in each aligned block of 8 rows (0 to 7, 8 to 15, ...) at most 2 rows name the same one
- route_gates: float32 [2048, 2], P(('ctx', 'exp')), may hold values from 0.2 to 1
- expert_gate: bfloat16 [16, 7168, 2048], P('exp', None, 'ctx'), may hold values from -0.0625 to 0.0625
- expert_up: bfloat16 [16, 7168, 2048], P('exp', None, 'ctx'), may hold values from -0.0625 to 0.0625
- expert_down: bfloat16 [16, 2048, 7168], P('exp', 'ctx'), may hold values from -0.125 to 0.125
Outputs:
- layer_out: bfloat16 [2048, 7168], P(('ctx', 'exp'))
Inputs may be any that keep to these rules, and one draw needn't show every extreme that they name: `expert_ids`: each token names 2 different experts. In every aligned block of 8 consecutive tokens no expert is named more than 2 times, a bound that some block reaches.
All inputs are finite; a program needn't handle non-finite values.
Results may differ from a plain program's by a relative error of at most 0.0085.
Values may be sent and summed in bfloat16 or wider, within the bound.
A program may use at most 128 MiB of HBM per device.

v0:
```python
import math
import jax
import jax.numpy as jnp
from jax import lax
from jax.sharding import PartitionSpec as P

WINDOW = 512
score_gain = 2.0
norm_eps = 1e-06


def passed_along(block, axis, distance):
    devices = range(lax.axis_size(axis))
    route = [(i - distance, i) for i in devices if i - distance in devices]
    return lax.ppermute(block, axis, route)


def head_norm(matrix, head_width):
    row_count = matrix.shape[0]
    shaped = matrix.reshape(row_count, -1, head_width).astype(jnp.float32)
    scaled = shaped * lax.rsqrt(jnp.mean(shaped * shaped, axis=2, keepdims=True) + norm_eps)
    return scaled.reshape(row_count, -1)


def compress(extended, position_weights, head_width):
    stride_len = position_weights.shape[0] // 2
    head_count = position_weights.shape[1]
    blocks = extended.reshape(-1, stride_len, head_count, head_width).astype(jnp.float32)
    first_half = jnp.einsum(
        "nshd,sh->nhd", blocks[:-1], position_weights[:stride_len], precision=lax.Precision.HIGHEST
    )
    second_half = jnp.einsum(
        "nshd,sh->nhd", blocks[1:], position_weights[stride_len:], precision=lax.Precision.HIGHEST
    )
    return (first_half + second_half).reshape(blocks.shape[0] - 1, head_count * head_width)


def local(
    query_input,
    key_input,
    value_input,
    gate_logits,
    comp_weight,
    out_proj,
    residual_in,
    ffn_gain,
    expert_ids,
    route_gates,
    expert_gate,
    expert_up,
    expert_down,
):
    row_count = query_input.shape[0]
    head_count = comp_weight.shape[2]
    head_width = query_input.shape[1] // head_count
    block_len = comp_weight.shape[1]
    stride_len = block_len // 2
    exp_count = lax.axis_size("exp")
    ctx_index = lax.axis_index("ctx")
    scale = score_gain / math.sqrt(head_width)
    query_norm = head_norm(query_input, head_width).astype(jnp.bfloat16)
    key_norm = head_norm(key_input, head_width).astype(jnp.bfloat16)
    next_keys, next_values = passed_along(
        (key_input[:stride_len], value_input[:stride_len]), "ctx", -1
    )
    comp_keys = head_norm(
        compress(jnp.concatenate([key_input, next_keys], 0), comp_weight[0], head_width), head_width
    ).astype(jnp.bfloat16)
    comp_values = compress(
        jnp.concatenate([value_input, next_values], 0), comp_weight[1], head_width
    ).astype(jnp.bfloat16)
    query_pos = ctx_index * row_count + jnp.arange(row_count, dtype=jnp.int32)
    query_heads = query_norm.reshape(row_count, head_count, head_width)
    part_keys = lax.all_gather(comp_keys, "ctx", axis=0, tiled=True)
    part_values = lax.all_gather(comp_values, "ctx", axis=0, tiled=True)
    part_count = part_keys.shape[0]
    scores = jnp.einsum(
        "thd,nhd->htn",
        query_heads,
        part_keys.reshape(part_count, head_count, head_width),
        preferred_element_type=jnp.float32,
    )
    block_end = jnp.arange(part_count, dtype=jnp.int32) * stride_len + block_len - 1
    visible = block_end[None, :] <= query_pos[:, None]
    weights = jnp.where(visible[None], jnp.exp(scale * scores), 0.0)
    running_total = jnp.sum(weights, axis=2).T
    collected = jnp.einsum(
        "htn,nhd->thd",
        weights.astype(jnp.bfloat16),
        part_values.reshape(part_count, head_count, head_width),
        preferred_element_type=jnp.float32,
    )
    cmp_sum = collected.reshape(row_count, -1)
    no_block = (query_pos < block_len - 1).astype(jnp.float32)
    cmp_out = (
        cmp_sum.reshape(row_count, head_count, head_width)
        / (running_total + no_block[:, None])[:, :, None]
    )
    shift_count = max(1, WINDOW // row_count)
    earlier_keys = []
    earlier_values = []
    for distance in range(shift_count, 0, -1):
        moved_keys, moved_values = passed_along((key_norm, value_input), "ctx", distance)
        earlier_keys.append(moved_keys)
        earlier_values.append(moved_values)
    near_keys = jnp.concatenate(earlier_keys + [key_norm], 0)
    near_values = jnp.concatenate(earlier_values + [value_input], 0)
    key_pos = ctx_index * row_count - WINDOW + jnp.arange(near_keys.shape[0], dtype=jnp.int32)
    near_scores = jnp.einsum(
        "thd,shd->hts",
        query_heads,
        near_keys.reshape(-1, head_count, head_width),
        preferred_element_type=jnp.float32,
    )
    inside = (
        (key_pos[None, :] <= query_pos[:, None])
        & (key_pos[None, :] > query_pos[:, None] - WINDOW)
        & (key_pos[None, :] >= 0)
    )
    near_weights = jnp.where(inside[None], jnp.exp(scale * near_scores), 0.0)
    win_total = jnp.sum(near_weights, axis=2).T
    win_sum = jnp.einsum(
        "hts,shd->thd",
        near_weights.astype(jnp.bfloat16),
        near_values.reshape(-1, head_count, head_width),
        preferred_element_type=jnp.float32,
    )
    win_out = win_sum / win_total[:, :, None]
    branch_gates = jax.nn.sigmoid(gate_logits)
    attended = (
        (branch_gates[0][:, :, None] * cmp_out + branch_gates[1][:, :, None] * win_out)
        .reshape(row_count, -1)
        .astype(jnp.bfloat16)
    )
    token_share = row_count // exp_count
    partial_sum = jnp.dot(
        attended,
        lax.all_gather(out_proj, "ctx", axis=1, tiled=True),
        preferred_element_type=jnp.float32,
    )
    projected = lax.psum_scatter(partial_sum, "exp", scatter_dimension=0, tiled=True)
    hidden_state = residual_in.astype(jnp.float32) + projected
    mean_square = jnp.mean(hidden_state * hidden_state, axis=1, keepdims=True)
    normed = (hidden_state * lax.rsqrt(mean_square + norm_eps) * ffn_gain).astype(jnp.bfloat16)
    model_width = normed.shape[1]
    top_count = expert_ids.shape[1]
    capacity = max(2, 2 * token_share * top_count // exp_count)
    flat_ids = expert_ids.reshape(-1)
    chosen = (flat_ids[:, None] == jnp.arange(exp_count, dtype=jnp.int32)[None, :]).astype(
        jnp.int32
    )
    slots = jnp.sum((jnp.cumsum(chosen, axis=0) - chosen) * chosen, axis=1)
    targets = (flat_ids * capacity + slots).reshape(token_share, top_count)
    slot_range = jnp.arange(exp_count * capacity, dtype=jnp.int32)
    dispatch_map = jnp.sum(
        (slot_range[:, None, None] == targets[None, :, :]).astype(jnp.float32), axis=2
    ).astype(jnp.bfloat16)
    outgoing = (
        jnp.dot(dispatch_map, normed, preferred_element_type=jnp.float32)
        .astype(jnp.bfloat16)
        .reshape(exp_count, capacity, model_width)
    )
    arrived = lax.all_to_all(outgoing, "exp", split_axis=0, concat_axis=0, tiled=True)
    gate_cols = expert_gate[0]
    up_cols = expert_up[0]
    down_rows = expert_down[0]
    portion = lax.all_gather(arrived, "ctx", axis=0, tiled=True)
    flat_rows = portion.reshape(-1, model_width)
    gate_part = jnp.dot(flat_rows, gate_cols, preferred_element_type=jnp.float32)
    up_part = jnp.dot(flat_rows, up_cols, preferred_element_type=jnp.float32)
    activated = (jax.nn.silu(gate_part) * up_part).astype(jnp.bfloat16)
    partial_out = jnp.dot(activated, down_rows, preferred_element_type=jnp.float32).reshape(
        portion.shape
    )
    finished = lax.psum_scatter(
        partial_out.astype(jnp.bfloat16), "ctx", scatter_dimension=0, tiled=True
    )
    returned = lax.all_to_all(finished, "exp", split_axis=0, concat_axis=0, tiled=True).reshape(
        -1, model_width
    )
    combine_map = jnp.sum(
        jnp.where(slot_range[None, None, :] == targets[:, :, None], route_gates[:, :, None], 0.0),
        axis=1,
    )
    moe_out = jnp.dot(combine_map, returned.astype(jnp.float32), precision=lax.Precision.HIGHEST)
    return (hidden_state + moe_out).astype(jnp.bfloat16)


def solution(mesh):
    in_specs = (
        P("ctx", "exp"),
        P("ctx", "exp"),
        P("ctx", "exp"),
        P(None, "ctx", "exp"),
        P(None, None, "exp"),
        P("exp", "ctx"),
        P(("ctx", "exp"), None),
        P(),
        P(("ctx", "exp"), None),
        P(("ctx", "exp"), None),
        P("exp", None, "ctx"),
        P("exp", None, "ctx"),
        P("exp", "ctx", None),
    )
    out_specs = P(("ctx", "exp"), None)
    return jax.shard_map(local, mesh=mesh, in_specs=in_specs, out_specs=out_specs, check_vma=False)
```

profile of v0, /device:TPU:8, one launch (start us, length us, event | category | flops | bytes accessed | tf_op | source)
XLA Modules:
  0.0 412.8 jit_solution(15140837322775450915)
XLA Ops:
  6.6 0.7 all-gather.3.cloned.1.call-update
  7.3 1.0 copy.91
  8.4 5.2 %collective-permute-start.6 = (bf16[128,512]{0,1:T(8,128)(2,1)S(1)}, bf16[128,512]{0,1:T(8,128)(2,1)S(1)}, u32[]{:S(2)}, u32[]{:S(2)}) collective-permute-start(bf16[128,512]{0,1:T(8,128)(2,1)S(1)} %fusion.24), channel_id=1, source_target_pairs={{0,64},{16,80},{32,96},{48,112},{64,128},{80,144},{96,160},{112,17... | collective-permute-start | bytes 393224 | tf_op jit(solution)/shard_map/ppermute | solution.py:15
  13.6 3.0 collective-permute-start.7
  16.6 5.0 %collective-permute-start.8 = (bf16[128,512]{0,1:T(8,128)(2,1)S(1)}, bf16[128,512]{0,1:T(8,128)(2,1)S(1)}, u32[]{:S(2)}, u32[]{:S(2)}) collective-permute-start(bf16[128,512]{0,1:T(8,128)(2,1)S(1)} %fusion.24), channel_id=1, source_target_pairs={{0,32},{16,48},{32,64},{48,80},{64,96},{80,112},{96,128},{112,144}... | collective-permute-start | bytes 393224 | tf_op jit(solution)/shard_map/ppermute | solution.py:15
  21.7 3.4 collective-permute-start.2
  25.1 1.3 slice.74
  26.4 1.3 collective-permute-start.1
  27.7 1.6 slice.71
  29.3 0.9 slice.63
  30.2 0.9 convert_multiply_fusion.3
  31.5 0.7 add_divide_fusion
  32.8 1.4 fusion.49
  34.3 0.8 and_and_fusion
  35.1 1.1 fusion.30
  36.3 0.8 fusion.34
  37.3 0.7 slice.66
  38.0 3.6 collective-permute-start.3
  42.1 18.2 %all_gather.13 = bf16[128,512]{1,0:T(8,128)(2,1)S(1)} all-gather(bf16[8,512]{1,0:T(8,128)(2,1)S(1)} %fusion.45), channel_id=1, replica_groups=mesh['ctx'=16,'exp'=16] {'ctx'}, dimensions={0}, use_global_device_ids=true | all-gather | bytes 139264 | tf_op jit(solution)/shard_map/all_gather | solution.py:74
  60.4 0.9 fusion.51
  61.3 2.9 collective-permute-start.4
  64.2 2.0 collective-permute-start.5
  66.2 4.5 %collective-permute-done.4 = bf16[128,512]{1,0:T(8,128)(2,1)S(1)} collective-permute-done((bf16[128,512]{1,0:T(8,128)(2,1)S(1)}, bf16[128,512]{1,0:T(8,128)(2,1)S(1)}, u32[]{:S(2)}, u32[]{:S(2)}) %collective-permute-start.4) | collective-permute-done | bytes 131104 | tf_op jit(solution)/shard_map/ppermute | solution.py:15
  70.8 1.9 collective-permute-start.9
  72.7 1.3 collective-permute-start
  74.1 4.0 collective-permute-done
  78.2 0.8 fusion.32
  79.0 0.7 fusion.44
  79.8 19.0 %all_gather.12 = bf16[128,512]{1,0:T(8,128)(2,1)S(1)} all-gather(bf16[8,512]{1,0:T(8,128)(2,1)S(1)} %fusion.44), channel_id=1, replica_groups=mesh['ctx'=16,'exp'=16] {'ctx'}, dimensions={0}, use_global_device_ids=true | all-gather | bytes 139264 | tf_op jit(solution)/shard_map/all_gather | solution.py:75
  99.3 0.7 constant_dynamic-update-slice_fusion.7
  100.0 1.6 constant_dynamic-update-slice_fusion.6
  101.6 0.7 constant_dynamic-update-slice_fusion.5
  102.3 1.7 fusion.50
  104.6 7.5 %fusion.52 = f32[128,7168]{1,0:T(8,128)} fusion(bf16[128,512]{0,1:T(8,128)(2,1)S(1)} %bitcast.126, bf16[512,7168]{0,1:T(8,128)(2,1)} %all-gather.3.cloned.1.call-done), kind=kOutput, calls=%fused_computation.101 | convolution fusion | flops 939524096 | bytes 11141120 | tf_op jit(solution)/shard_map/dot_general | solution.py:136
  114.8 107.4 %all-reduce.3.cloned.1.call-done = f32[128,7168]{1,0:T(8,128)} async-done(((f32[128,7168]{1,0:T(8,128)}), f32[128,7168]{1,0:T(8,128)}) %all-reduce.3.cloned.1.call-update) | async-done | bytes 3670032
  222.1 1.1 multiply_reduce_fusion
  223.3 1.3 convolution_convert_fusion.1
  224.7 15.1 %all_to_all.10 = bf16[16,2,7168]{2,1,0:T(2,128)(2,1)} all-to-all(bf16[16,2,7168]{2,1,0:T(2,128)(2,1)S(1)} %reshape.231), channel_id=1, replica_groups=mesh['ctx'=16,'exp'=16] {'exp'}, dimensions={0} | all-to-all | bytes 917504 | tf_op jit(solution)/shard_map/all_to_all | solution.py:163
  240.1 49.7 %all-gather.5.cloned.1.call-done = bf16[256,2,7168]{2,1,0:T(2,128)(2,1)} async-done(((bf16[16,2,7168]{2,1,0:T(2,128)(2,1)}), bf16[256,2,7168]{2,1,0:T(2,128)(2,1)}) %all-gather.5.cloned.1.call-update) | async-done | bytes 7340048 | tf_op jit(solution)/shard_map/all_gather | solution.py:167
  289.8 15.4 %reshape.232 = bf16[512,7168]{1,0:T(8,128)(2,1)} reshape(bf16[256,2,7168]{2,1,0:T(2,128)(2,1)} %all-gather.5.cloned.1.call-done) | data formatting | bytes 14680064 | tf_op jit(solution)/shard_map/reshape | solution.py:168
  305.2 5.8 %fusion.4 = f32[512,128]{1,0:T(8,128)S(1)} fusion(bf16[512,7168]{1,0:T(8,128)(2,1)} %reshape.232, bf16[1,7168,128]{2,1,0:T(8,128)(2,1)} %param.23), kind=kOutput, calls=%fused_computation.7 | convolution fusion | flops 939524096 | bytes 9437184 | tf_op jit(solution)/shard_map/dot_general | solution.py:169
  311.4 2.1 fusion.19
  313.4 5.0 %convolution_convert_fusion = bf16[256,2,7168]{2,0,1:T(8,128)(2,1)} fusion(bf16[1,128,7168]{2,1,0:T(8,128)(2,1)S(1)} %copy-done, bf16[256,2,128]{2,1,0:T(2,128)(2,1)S(1)} %bitcast.127), kind=kOutput, calls=%fused_computation | convolution fusion | flops 943194112 | bytes 9306112 | tf_op jit(solution)/shard_map/dot_general | solution.py:172
  318.5 67.8 %reduce-scatter.2.cloned.1.call-done = bf16[16,2,7168]{2,0,1:T(8,128)(2,1)} async-done(((bf16[256,2,7168]{2,0,1:T(8,128)(2,1)}), bf16[16,2,7168]{2,0,1:T(8,128)(2,1)}) %reduce-scatter.2.cloned.1.call-update) | async-done | bytes 458768 | tf_op jit(solution)/shard_map/reduce_scatter | solution.py:175
  386.3 2.3 copy.99
  388.6 7.3 %all-to-all-start.1 = ((bf16[16,2,7168]{2,1,0:T(2,128)(2,1)}), bf16[16,2,7168]{2,1,0:T(2,128)(2,1)S(1)}, u32[]{:S(2)}, u32[]{:S(2)}) async-start(bf16[16,2,7168]{2,1,0:T(2,128)(2,1)} %copy.99), calls=%async_computation.2 | async-start | bytes 917504 | tf_op jit(solution)/shard_map/all_to_all | solution.py:178
  395.9 8.3 %all-to-all-done.1 = bf16[16,2,7168]{2,1,0:T(2,128)(2,1)S(1)} async-done(((bf16[16,2,7168]{2,1,0:T(2,128)(2,1)}), bf16[16,2,7168]{2,1,0:T(2,128)(2,1)S(1)}, u32[]{:S(2)}, u32[]{:S(2)}) %all-to-all-start.1) | async-done | bytes 458784 | tf_op jit(solution)/shard_map/all_to_all | solution.py:178
  404.4 1.9 fusion
  (98 shorter events, 6.2 us)
Async XLA Ops:
  6.5 306.9 %copy-start = (bf16[1,128,7168]{2,1,0:T(8,128)(2,1)S(1)}, bf16[1,128,7168]{2,1,0:T(8,128)(2,1)}, u32[]{:S(2)}) copy-start(bf16[1,128,7168]{2,1,0:T(8,128)(2,1)} %param.25) | copy-start | bytes 5505028
  6.5 35.1 %copy-start.2 = (bf16[128,512]{1,0:T(8,128)(2,1)S(1)}, bf16[128,512]{1,0:T(8,128)(2,1)}, u32[]{:S(2)}) copy-start(bf16[128,512]{1,0:T(8,128)(2,1)} %param.14) | copy-start | bytes 393220
  6.5 30.8 %copy-start.4 = (bf16[128,512]{1,0:T(8,128)(2,1)S(1)}, bf16[128,512]{1,0:T(8,128)(2,1)}, u32[]{:S(2)}) copy-start(bf16[128,512]{1,0:T(8,128)(2,1)} %param.15) | copy-start | bytes 393220
  6.5 30.7 %copy-start.5 = (bf16[128,512]{1,0:T(8,128)(2,1)S(1)}, bf16[128,512]{1,0:T(8,128)(2,1)}, u32[]{:S(2)}) copy-start(bf16[128,512]{1,0:T(8,128)(2,1)} %param.13) | copy-start | bytes 393220
  6.5 98.1 %all-gather.3.cloned.1.call-start = ((), (), s32[]{:S(2)}) async-start(), calls=%async_computation.3 | async-start | bytes 7798784 | tf_op jit(solution)/shard_map/all_gather | solution.py:138
  7.3 214.9 %all-reduce.3.cloned.1.call-start = ((), (), s32[]{:S(2)}) async-start(), calls=%async_computation.6 | async-start | bytes 7340032
  8.4 71.3 %collective-permute-start.6 = (bf16[128,512]{0,1:T(8,128)(2,1)S(1)}, bf16[128,512]{0,1:T(8,128)(2,1)S(1)}, u32[]{:S(2)}, u32[]{:S(2)}) collective-permute-start(bf16[128,512]{0,1:T(8,128)(2,1)S(1)} %fusion.24), channel_id=1, source_target_pairs={{0,64},{16,80},{32,96},{48,112},{64,128},{80,144},{96,160},{112,17... | collective-permute-start | bytes 393224 | tf_op jit(solution)/shard_map/ppermute | solution.py:15
  13.6 66.2 %collective-permute-start.7 = (bf16[128,512]{0,1:T(8,128)(2,1)S(1)}, bf16[128,512]{0,1:T(8,128)(2,1)S(1)}, u32[]{:S(2)}, u32[]{:S(2)}) collective-permute-start(bf16[128,512]{0,1:T(8,128)(2,1)S(1)} %fusion.24), channel_id=1, source_target_pairs={{0,48},{16,64},{32,80},{48,96},{64,112},{80,128},{96,144},{112,160... | collective-permute-start | bytes 393224 | tf_op jit(solution)/shard_map/ppermute | solution.py:15
  16.6 82.7 %collective-permute-start.8 = (bf16[128,512]{0,1:T(8,128)(2,1)S(1)}, bf16[128,512]{0,1:T(8,128)(2,1)S(1)}, u32[]{:S(2)}, u32[]{:S(2)}) collective-permute-start(bf16[128,512]{0,1:T(8,128)(2,1)S(1)} %fusion.24), channel_id=1, source_target_pairs={{0,32},{16,48},{32,64},{48,80},{64,96},{80,112},{96,128},{112,144}... | collective-permute-start | bytes 393224 | tf_op jit(solution)/shard_map/ppermute | solution.py:15
  21.7 39.6 %collective-permute-start.2 = (bf16[128,512]{1,0:T(8,128)(2,1)}, bf16[128,512]{1,0:T(8,128)(2,1)S(1)}, u32[]{:S(2)}, u32[]{:S(2)}) collective-permute-start(bf16[128,512]{1,0:T(8,128)(2,1)} %param.15), channel_id=1, source_target_pairs={{0,64},{16,80},{32,96},{48,112},{64,128},{80,144},{96,160},{112,17... | collective-permute-start | bytes 393224 | tf_op jit(solution)/shard_map/ppermute | solution.py:15
  26.4 11.6 %collective-permute-start.1 = (bf16[16,512]{1,0:T(8,128)(2,1)}, bf16[16,512]{1,0:T(8,128)(2,1)S(1)}, u32[]{:S(2)}, u32[]{:S(2)}) collective-permute-start(bf16[16,512]{1,0:T(8,128)(2,1)} %slice.74), channel_id=1, source_target_pairs={{16,0},{32,16},{48,32},{64,48},{80,64},{96,80},{112,96},{128,112},... | collective-permute-start | bytes 49160 | tf_op jit(solution)/shard_map/ppermute | solution.py:15
  37.3 24.0 %copy-start.6 = (bf16[16,4,8,128]{3,2,1,0:T(8,128)(2,1)}, bf16[16,4,8,128]{3,2,1,0:T(8,128)(2,1)S(1)}, u32[]{:S(2)}) copy-start(bf16[16,4,8,128]{3,2,1,0:T(8,128)(2,1)S(1)} %fusion.25) | copy-start | bytes 393220
  38.0 26.2 %collective-permute-start.3 = (bf16[128,512]{1,0:T(8,128)(2,1)S(1)}, bf16[128,512]{1,0:T(8,128)(2,1)S(1)}, u32[]{:S(2)}, u32[]{:S(2)}) collective-permute-start(bf16[128,512]{1,0:T(8,128)(2,1)S(1)} %copy-done.4), channel_id=1, source_target_pairs={{0,48},{16,64},{32,80},{48,96},{64,112},{80,128},{96,144},{112,160... | collective-permute-start | bytes 393224 | tf_op jit(solution)/shard_map/ppermute | solution.py:15
  61.3 42.7 %copy-start.10 = (f32[128,4]{0,1:T(4,128)S(1)}, f32[128,4]{0,1:T(4,128)}, u32[]{:S(2)}) copy-start(f32[128,4]{0,1:T(4,128)} %get-tuple-element.8) | copy-start | bytes 6148
  61.3 9.5 %collective-permute-start.4 = (bf16[128,512]{1,0:T(8,128)(2,1)S(1)}, bf16[128,512]{1,0:T(8,128)(2,1)S(1)}, u32[]{:S(2)}, u32[]{:S(2)}) collective-permute-start(bf16[128,512]{1,0:T(8,128)(2,1)S(1)} %copy-done.4), channel_id=1, source_target_pairs={{0,32},{16,48},{32,64},{48,80},{64,96},{80,112},{96,128},{112,144}... | collective-permute-start | bytes 393224 | tf_op jit(solution)/shard_map/ppermute | solution.py:15
  64.2 8.5 %collective-permute-start.5 = (bf16[128,512]{1,0:T(8,128)(2,1)S(1)}, bf16[128,512]{1,0:T(8,128)(2,1)S(1)}, u32[]{:S(2)}, u32[]{:S(2)}) collective-permute-start(bf16[128,512]{1,0:T(8,128)(2,1)S(1)} %copy-done.4), channel_id=1, source_target_pairs={{0,16},{16,32},{32,48},{48,64},{64,80},{80,96},{96,112},{112,128},... | collective-permute-start | bytes 393224 | tf_op jit(solution)/shard_map/ppermute | solution.py:15
  70.8 29.3 %collective-permute-start.9 = (bf16[128,512]{0,1:T(8,128)(2,1)S(1)}, bf16[128,512]{0,1:T(8,128)(2,1)}, u32[]{:S(2)}, u32[]{:S(2)}) collective-permute-start(bf16[128,512]{0,1:T(8,128)(2,1)S(1)} %fusion.24), channel_id=1, source_target_pairs={{0,16},{16,32},{32,48},{48,64},{64,80},{80,96},{96,112},{112,128},... | collective-permute-start | bytes 393224 | tf_op jit(solution)/shard_map/ppermute | solution.py:15
  72.7 5.4 %collective-permute-start = (bf16[16,512]{1,0:T(8,128)(2,1)}, bf16[16,512]{1,0:T(8,128)(2,1)S(1)}, u32[]{:S(2)}, u32[]{:S(2)}) collective-permute-start(bf16[16,512]{1,0:T(8,128)(2,1)} %slice.66), channel_id=1, source_target_pairs={{16,0},{32,16},{48,32},{64,48},{80,64},{96,80},{112,96},{128,112},... | collective-permute-start | bytes 49160 | tf_op jit(solution)/shard_map/ppermute | solution.py:15
  79.8 24.6 %copy-start.9 = (f32[128,4]{0,1:T(4,128)S(1)}, f32[128,4]{0,1:T(4,128)}, u32[]{:S(2)}) copy-start(f32[128,4]{0,1:T(4,128)} %get-tuple-element.7) | copy-start | bytes 6148
  79.8 19.1 %copy-start.8 = (bf16[640,512]{0,1:T(8,128)(2,1)}, bf16[640,512]{0,1:T(8,128)(2,1)S(1)}, u32[]{:S(2)}) copy-start(bf16[640,512]{0,1:T(8,128)(2,1)S(1)} %constant_dynamic-update-slice_fusion.8) | copy-start | bytes 1966084
  99.2 5.2 %copy-start.15 = (bf16[4,128,128]{1,2,0:T(8,128)(2,1)S(1)}, bf16[4,128,128]{1,2,0:T(8,128)(2,1)}, u32[]{:S(2)}) copy-start(bf16[4,128,128]{1,2,0:T(8,128)(2,1)} %get-tuple-element.16) | copy-start | bytes 393220
  112.1 0.7 copy-start.11
  112.1 1.3 copy-start.14
  112.1 110.0 %copy-start.3 = (bf16[8,7168]{1,0:T(8,128)(2,1)S(1)}, bf16[8,7168]{1,0:T(8,128)(2,1)}, u32[]{:S(2)}) copy-start(bf16[8,7168]{1,0:T(8,128)(2,1)} %param.19) | copy-start | bytes 344068
  112.1 111.1 %copy-start.7 = (f32[7168]{0:T(1024)S(1)}, f32[7168]{0:T(1024)}, u32[]{:S(2)}) copy-start(f32[7168]{0:T(1024)} %param.20) | copy-start | bytes 86020
  112.2 177.6 %all-gather.5.cloned.1.call-start = ((), (), s32[]{:S(2)}) async-start(), calls=%async_computation.4 | async-start | bytes 7798784 | tf_op jit(solution)/shard_map/all_gather | solution.py:167
  239.8 146.4 %reduce-scatter.2.cloned.1.call-start = ((), (), s32[]{:S(2)}) async-start(), calls=%async_computation.5 | async-start | bytes 7798784 | tf_op jit(solution)/shard_map/reduce_scatter | solution.py:175
  305.2 5.8 %copy-start.1 = (bf16[512,7168]{1,0:T(8,128)(2,1)S(1)}, bf16[512,7168]{1,0:T(8,128)(2,1)}, u32[]{:S(2)}) copy-start(bf16[512,7168]{1,0:T(8,128)(2,1)} %reshape.232) | copy-start | bytes 22020100
  305.2 6.2 %copy-start.13 = (bf16[1,7168,128]{2,1,0:T(8,128)(2,1)S(1)}, bf16[1,7168,128]{2,1,0:T(8,128)(2,1)}, u32[]{:S(2)}) copy-start(bf16[1,7168,128]{2,1,0:T(8,128)(2,1)} %param.24) | copy-start | bytes 5505028
  318.4 77.4 %copy-start.12 = (f32[8,2]{0,1:T(2,128)S(1)}, f32[8,2]{0,1:T(2,128)}, u32[]{:S(2)}) copy-start(f32[8,2]{0,1:T(2,128)} %param.22) | copy-start | bytes 196
  388.6 15.6 %all-to-all-start.1 = ((bf16[16,2,7168]{2,1,0:T(2,128)(2,1)}), bf16[16,2,7168]{2,1,0:T(2,128)(2,1)S(1)}, u32[]{:S(2)}, u32[]{:S(2)}) async-start(bf16[16,2,7168]{2,1,0:T(2,128)(2,1)} %copy.99), calls=%async_computation.2 | async-start | bytes 917504 | tf_op jit(solution)/shard_map/all_to_all | solution.py:178
Sparse Core Ops, SparseCore 0:
  9.2 68.1 all-gather.2
  112.3 109.8 all-reduce.2
  240.0 49.7 all-gather.4
  318.6 67.6 reduce-scatter.1
where the time goes:
time: 414 us; the launch traced here: 413 us
  waiting for transfers between devices  243 us (59%)
  blocking collectives  52.3 us (13%)
  starting transfers between devices  37.2 us (9%)
  local copies, waits for them, and re-layouts  31.5 us (8%)
  matrix products  29.6 us (7%)
  between operations  14.3 us (3%)
  other arithmetic  5.39 us (1%)
    unnamed x5, waiting for transfers between devices  108 us
    reduce_scatter x1, waiting for transfers between devices, local(): lax.psum_scatter(partial_out.astype(jnp.bfloat16), 'ctx', scatter_dimensi...  67.8 us
    all_gather x1, waiting for transfers between devices, local(): portion = lax.all_gather(arrived, 'ctx', axis=0, tiled=True)  49.7 us
    ppermute x10, starting transfers between devices, passed_along(): return lax.ppermute(block, axis, route)  29.6 us
    all_gather x1, blocking collectives, local(): part_values = lax.all_gather(comp_values, 'ctx', axis=0, tiled=True)  19 us
    all_gather x1, blocking collectives, local(): part_keys = lax.all_gather(comp_keys, 'ctx', axis=0, tiled=True)  18.2 us
    reshape x1, local copies, waits for them, and re-layouts, local(): flat_rows = portion.reshape(-1, model_width)  15.4 us
    all_to_all x1, blocking collectives, local(): lax.all_to_all(outgoing, 'exp', split_axis=0, concat_axis=0, tiled=True)  15.1 us
  transfers between devices with their start and end apart: 15, of which 6 were waited for; matrix products, arithmetic and copies ran while one was open for 6% of the time, Pallas kernels for 0%

commit v1 on v0

--- a/solution.py
+++ b/solution.py
@@ -164,7 +164,13 @@
     gate_cols = expert_gate[0]
     up_cols = expert_up[0]
     down_rows = expert_down[0]
-    portion = lax.all_gather(arrived, "ctx", axis=0, tiled=True)
+    view_out = lax.all_to_all(
+        jnp.stack([arrived for _ in range(lax.axis_size("ctx"))]),
+        axis_name="ctx",
+        split_axis=0,
+        concat_axis=0,
+    )
+    portion = jnp.concatenate(view_out, axis=0)
     flat_rows = portion.reshape(-1, model_width)
     gate_part = jnp.dot(flat_rows, gate_cols, preferred_element_type=jnp.float32)
     up_part = jnp.dot(flat_rows, up_cols, preferred_element_type=jnp.float32)

time: 414 us -> 537 us (1.30)
  blocking collectives: 52.3 us -> 221 us
  waiting for transfers between devices: 243 us -> 190 us
  local copies, waits for them, and re-layouts: 31.5 us -> 37.8 us
    all_to_all x0 -> x1, blocking collectives: none -> 169 us  [local(): lax.all_to_all(jnp.stack([arrived for _ in range(lax.axis_size('ctx'))]),...]
    all_gather x1 -> x0, waiting for transfers between devices: 49.7 us -> none  [local(): portion = lax.all_gather(arrived, 'ctx', axis=0, tiled=True)]
    another operation x0 -> x2, local copies, waits for them, and re-layouts: none -> 21.7 us  [the longest x1 15.4 us: local(): flat_rows = portion.reshape(-1, model_width)]
    reshape x1 -> x0, local copies, waits for them, and re-layouts: 15.4 us -> none  [local(): flat_rows = portion.reshape(-1, model_width)]
    unnamed x5 -> x4, waiting for transfers between devices: 108 us -> 108 us
  transfers between devices with their start and end apart: 15 -> 14, of which waited for: 6 -> 5; matrix products, arithmetic and copies ran while one was open for 6% -> 4% of each run, Pallas kernels for 0% -> 0%
where the time goes in v1:
time: 537 us; the launch traced here: 535 us
  blocking collectives  221 us (41%)
  waiting for transfers between devices  190 us (35%)
  local copies, waits for them, and re-layouts  37.8 us (7%)
  starting transfers between devices  37 us (7%)
  matrix products  29.6 us (6%)
  between operations  14.3 us (3%)
  other arithmetic  5.38 us (1%)
    all_to_all x1, blocking collectives, local(): lax.all_to_all(jnp.stack([arrived for _ in range(lax.axis_size('ctx'))]),...  169 us
    unnamed x4, waiting for transfers between devices  108 us
    reduce_scatter x1, waiting for transfers between devices, local(): lax.psum_scatter(partial_out.astype(jnp.bfloat16), 'ctx', scatter_dimensi...  65.1 us
    ppermute x10, starting transfers between devices, passed_along(): return lax.ppermute(block, axis, route)  29.6 us
    all_gather x1, blocking collectives, local(): part_values = lax.all_gather(comp_values, 'ctx', axis=0, tiled=True)  19.1 us
    all_gather x1, blocking collectives, local(): part_keys = lax.all_gather(comp_keys, 'ctx', axis=0, tiled=True)  18.2 us
    another operation x1, local copies, waits for them, and re-layouts, local(): flat_rows = portion.reshape(-1, model_width)  15.4 us
    all_to_all x1, blocking collectives, local(): lax.all_to_all(outgoing, 'exp', split_axis=0, concat_axis=0, tiled=True)  15 us
  transfers between devices with their start and end apart: 14, of which 5 were waited for; matrix products, arithmetic and copies ran while one was open for 4% of the time, Pallas kernels for 0%

profile of v1, /device:TPU:8, one launch (start us, length us, event | category | flops | bytes accessed | tf_op | source)
XLA Modules:
  0.0 535.4 jit_solution(12682539696160982535)
XLA Ops:
  6.6 0.7 all-gather.2.cloned.1.call-update
  7.3 1.0 copy.91
  8.4 5.2 collective-permute-start.6
  13.6 3.0 collective-permute-start.7
  16.6 5.0 collective-permute-start.8
  21.7 3.4 collective-permute-start.2
  25.1 1.3 slice.74
  26.4 1.3 collective-permute-start.1
  27.7 1.6 slice.71
  29.3 0.9 slice.63
  30.2 0.9 convert_multiply_fusion.3
  31.5 0.7 add_divide_fusion
  32.8 1.4 fusion.49
  34.3 0.8 and_and_fusion
  35.1 1.1 fusion.30
  36.3 0.8 fusion.34
  38.0 3.6 collective-permute-start.3
  42.1 18.2 %all_gather.10 = bf16[128,512]{1,0:T(8,128)(2,1)S(1)} all-gather(bf16[8,512]{1,0:T(8,128)(2,1)S(1)} %fusion.45), channel_id=1, replica_groups=mesh['ctx'=16,'exp'=16] {'ctx'}, dimensions={0}, use_global_device_ids=true | all-gather | bytes 139264 | tf_op jit(solution)/shard_map/all_gather | solution.py:74
  60.4 0.9 fusion.51
  61.4 2.9 collective-permute-start.4
  64.3 2.0 collective-permute-start.5
  66.3 4.4 collective-permute-done.4
  70.7 2.0 collective-permute-start.9
  72.7 1.3 collective-permute-start
  74.0 4.0 collective-permute-done
  78.1 0.9 fusion.32
  79.0 0.7 fusion.44
  79.8 19.1 %all_gather.9 = bf16[128,512]{1,0:T(8,128)(2,1)S(1)} all-gather(bf16[8,512]{1,0:T(8,128)(2,1)S(1)} %fusion.44), channel_id=1, replica_groups=mesh['ctx'=16,'exp'=16] {'ctx'}, dimensions={0}, use_global_device_ids=true | all-gather | bytes 139264 | tf_op jit(solution)/shard_map/all_gather | solution.py:75
  99.4 0.7 constant_dynamic-update-slice_fusion.7
  100.1 1.6 constant_dynamic-update-slice_fusion.6
  101.6 0.7 constant_dynamic-update-slice_fusion.5
  102.3 1.7 fusion.50
  104.6 7.5 %fusion.52 = f32[128,7168]{1,0:T(8,128)} fusion(bf16[128,512]{0,1:T(8,128)(2,1)S(1)} %bitcast.126, bf16[512,7168]{0,1:T(8,128)(2,1)} %all-gather.2.cloned.1.call-done), kind=kOutput, calls=%fused_computation.101 | convolution fusion | flops 939524096 | bytes 11141120 | tf_op jit(solution)/shard_map/dot_general | solution.py:136
  114.7 107.4 %all-reduce.3.cloned.1.call-done = f32[128,7168]{1,0:T(8,128)} async-done(((f32[128,7168]{1,0:T(8,128)}), f32[128,7168]{1,0:T(8,128)}) %all-reduce.3.cloned.1.call-update) | async-done | bytes 3670032
  222.1 1.1 multiply_reduce_fusion
  223.3 1.3 convolution_convert_fusion.1
  224.7 15.0 %all_to_all.15 = bf16[16,2,7168]{2,1,0:T(2,128)(2,1)S(1)} all-to-all(bf16[16,2,7168]{2,1,0:T(2,128)(2,1)S(1)} %reshape.230), channel_id=1, replica_groups=mesh['ctx'=16,'exp'=16] {'exp'}, dimensions={0} | all-to-all | bytes 917504 | tf_op jit(solution)/shard_map/all_to_all | solution.py:163
  239.7 6.3 %stack.2 = bf16[16,16,2,7168]{3,2,1,0:T(2,128)(2,1)S(1)} broadcast(bf16[16,2,7168]{2,1,0:T(2,128)(2,1)S(1)} %all_to_all.15), dimensions={1,2,3} | broadcast | bytes 7798784 | tf_op jit(solution)/shard_map/stack | solution.py:168
  246.0 169.0 %all_to_all.16 = bf16[16,16,2,7168]{3,2,1,0:T(2,128)(2,1)} all-to-all(bf16[16,16,2,7168]{3,2,1,0:T(2,128)(2,1)S(1)} %stack.2), channel_id=1, replica_groups=mesh['ctx'=16,'exp'=16] {'ctx'}, dimensions={0} | all-to-all | bytes 14680064 | tf_op jit(solution)/shard_map/all_to_all | solution.py:167
  415.0 15.4 %reshape_reshape.3 = bf16[512,7168]{1,0:T(8,128)(2,1)} reshape(bf16[16,16,2,7168]{3,2,1,0:T(2,128)(2,1)} %all_to_all.16) | data formatting | bytes 14680064 | tf_op jit(solution)/shard_map/reshape;reshape | solution.py:174
  430.5 5.8 %fusion.4 = f32[512,128]{1,0:T(8,128)S(1)} fusion(bf16[512,7168]{1,0:T(8,128)(2,1)} %reshape_reshape.3, bf16[1,7168,128]{2,1,0:T(8,128)(2,1)} %param.23), kind=kOutput, calls=%fused_computation.7 | convolution fusion | flops 939524096 | bytes 9437184 | tf_op jit(solution)/shard_map/dot_general | solution.py:175
  436.7 2.1 fusion.19
  438.7 5.0 convolution_convert_fusion
  443.8 65.1 %reduce-scatter.2.cloned.1.call-done = bf16[16,2,7168]{2,0,1:T(8,128)(2,1)} async-done(((bf16[256,2,7168]{2,0,1:T(8,128)(2,1)}), bf16[16,2,7168]{2,0,1:T(8,128)(2,1)}) %reduce-scatter.2.cloned.1.call-update) | async-done | bytes 458768 | tf_op jit(solution)/shard_map/reduce_scatter | solution.py:181
  508.8 2.3 copy.99
  511.1 7.3 %all-to-all-start.2 = ((bf16[16,2,7168]{2,1,0:T(2,128)(2,1)}), bf16[16,2,7168]{2,1,0:T(2,128)(2,1)S(1)}, u32[]{:S(2)}, u32[]{:S(2)}) async-start(bf16[16,2,7168]{2,1,0:T(2,128)(2,1)} %copy.99), calls=%async_computation.3 | async-start | bytes 917504 | tf_op jit(solution)/shard_map/all_to_all | solution.py:184
  518.5 8.3 %all-to-all-done.2 = bf16[16,2,7168]{2,1,0:T(2,128)(2,1)S(1)} async-done(((bf16[16,2,7168]{2,1,0:T(2,128)(2,1)}), bf16[16,2,7168]{2,1,0:T(2,128)(2,1)S(1)}, u32[]{:S(2)}, u32[]{:S(2)}) %all-to-all-start.2) | async-done | bytes 458784 | tf_op jit(solution)/shard_map/all_to_all | solution.py:184
  526.9 1.9 fusion
  (97 shorter events, 6.6 us)
Async XLA Ops:
  6.5 432.2 %copy-start = (bf16[1,128,7168]{2,1,0:T(8,128)(2,1)S(1)}, bf16[1,128,7168]{2,1,0:T(8,128)(2,1)}, u32[]{:S(2)}) copy-start(bf16[1,128,7168]{2,1,0:T(8,128)(2,1)} %param.25) | copy-start | bytes 5505028
  6.5 35.1 %copy-start.2 = (bf16[128,512]{1,0:T(8,128)(2,1)S(1)}, bf16[128,512]{1,0:T(8,128)(2,1)}, u32[]{:S(2)}) copy-start(bf16[128,512]{1,0:T(8,128)(2,1)} %param.14) | copy-start | bytes 393220
  6.5 30.8 %copy-start.4 = (bf16[128,512]{1,0:T(8,128)(2,1)S(1)}, bf16[128,512]{1,0:T(8,128)(2,1)}, u32[]{:S(2)}) copy-start(bf16[128,512]{1,0:T(8,128)(2,1)} %param.15) | copy-start | bytes 393220
  6.5 30.7 %copy-start.5 = (bf16[128,512]{1,0:T(8,128)(2,1)S(1)}, bf16[128,512]{1,0:T(8,128)(2,1)}, u32[]{:S(2)}) copy-start(bf16[128,512]{1,0:T(8,128)(2,1)} %param.13) | copy-start | bytes 393220
  6.5 98.0 %all-gather.2.cloned.1.call-start = ((), (), s32[]{:S(2)}) async-start(), calls=%async_computation.4 | async-start | bytes 7798784 | tf_op jit(solution)/shard_map/all_gather | solution.py:138
  7.3 214.9 %all-reduce.3.cloned.1.call-start = ((), (), s32[]{:S(2)}) async-start(), calls=%async_computation.6 | async-start | bytes 7340032
  8.4 71.2 %collective-permute-start.6 = (bf16[128,512]{0,1:T(8,128)(2,1)S(1)}, bf16[128,512]{0,1:T(8,128)(2,1)S(1)}, u32[]{:S(2)}, u32[]{:S(2)}) collective-permute-start(bf16[128,512]{0,1:T(8,128)(2,1)S(1)} %fusion.24), channel_id=1, source_target_pairs={{0,64},{16,80},{32,96},{48,112},{64,128},{80,144},{96,160},{112,17... | collective-permute-start | bytes 393224 | tf_op jit(solution)/shard_map/ppermute | solution.py:15
  13.6 66.1 %collective-permute-start.7 = (bf16[128,512]{0,1:T(8,128)(2,1)S(1)}, bf16[128,512]{0,1:T(8,128)(2,1)S(1)}, u32[]{:S(2)}, u32[]{:S(2)}) collective-permute-start(bf16[128,512]{0,1:T(8,128)(2,1)S(1)} %fusion.24), channel_id=1, source_target_pairs={{0,48},{16,64},{32,80},{48,96},{64,112},{80,128},{96,144},{112,160... | collective-permute-start | bytes 393224 | tf_op jit(solution)/shard_map/ppermute | solution.py:15
  16.6 82.7 %collective-permute-start.8 = (bf16[128,512]{0,1:T(8,128)(2,1)S(1)}, bf16[128,512]{0,1:T(8,128)(2,1)S(1)}, u32[]{:S(2)}, u32[]{:S(2)}) collective-permute-start(bf16[128,512]{0,1:T(8,128)(2,1)S(1)} %fusion.24), channel_id=1, source_target_pairs={{0,32},{16,48},{32,64},{48,80},{64,96},{80,112},{96,128},{112,144}... | collective-permute-start | bytes 393224 | tf_op jit(solution)/shard_map/ppermute | solution.py:15
  21.7 39.7 %collective-permute-start.2 = (bf16[128,512]{1,0:T(8,128)(2,1)}, bf16[128,512]{1,0:T(8,128)(2,1)S(1)}, u32[]{:S(2)}, u32[]{:S(2)}) collective-permute-start(bf16[128,512]{1,0:T(8,128)(2,1)} %param.15), channel_id=1, source_target_pairs={{0,64},{16,80},{32,96},{48,112},{64,128},{80,144},{96,160},{112,17... | collective-permute-start | bytes 393224 | tf_op jit(solution)/shard_map/ppermute | solution.py:15
  26.4 11.6 %collective-permute-start.1 = (bf16[16,512]{1,0:T(8,128)(2,1)}, bf16[16,512]{1,0:T(8,128)(2,1)S(1)}, u32[]{:S(2)}, u32[]{:S(2)}) collective-permute-start(bf16[16,512]{1,0:T(8,128)(2,1)} %slice.74), channel_id=1, source_target_pairs={{16,0},{32,16},{48,32},{64,48},{80,64},{96,80},{112,96},{128,112},... | collective-permute-start | bytes 49160 | tf_op jit(solution)/shard_map/ppermute | solution.py:15
  37.3 24.0 %copy-start.6 = (bf16[16,4,8,128]{3,2,1,0:T(8,128)(2,1)}, bf16[16,4,8,128]{3,2,1,0:T(8,128)(2,1)S(1)}, u32[]{:S(2)}) copy-start(bf16[16,4,8,128]{3,2,1,0:T(8,128)(2,1)S(1)} %fusion.25) | copy-start | bytes 393220
  38.0 26.3 %collective-permute-start.3 = (bf16[128,512]{1,0:T(8,128)(2,1)S(1)}, bf16[128,512]{1,0:T(8,128)(2,1)S(1)}, u32[]{:S(2)}, u32[]{:S(2)}) collective-permute-start(bf16[128,512]{1,0:T(8,128)(2,1)S(1)} %copy-done.4), channel_id=1, source_target_pairs={{0,48},{16,64},{32,80},{48,96},{64,112},{80,128},{96,144},{112,160... | collective-permute-start | bytes 393224 | tf_op jit(solution)/shard_map/ppermute | solution.py:15
  61.3 42.6 %copy-start.10 = (f32[128,4]{0,1:T(4,128)S(1)}, f32[128,4]{0,1:T(4,128)}, u32[]{:S(2)}) copy-start(f32[128,4]{0,1:T(4,128)} %get-tuple-element.8) | copy-start | bytes 6148
  61.4 9.4 %collective-permute-start.4 = (bf16[128,512]{1,0:T(8,128)(2,1)S(1)}, bf16[128,512]{1,0:T(8,128)(2,1)S(1)}, u32[]{:S(2)}, u32[]{:S(2)}) collective-permute-start(bf16[128,512]{1,0:T(8,128)(2,1)S(1)} %copy-done.4), channel_id=1, source_target_pairs={{0,32},{16,48},{32,64},{48,80},{64,96},{80,112},{96,128},{112,144}... | collective-permute-start | bytes 393224 | tf_op jit(solution)/shard_map/ppermute | solution.py:15
  64.3 8.4 %collective-permute-start.5 = (bf16[128,512]{1,0:T(8,128)(2,1)S(1)}, bf16[128,512]{1,0:T(8,128)(2,1)S(1)}, u32[]{:S(2)}, u32[]{:S(2)}) collective-permute-start(bf16[128,512]{1,0:T(8,128)(2,1)S(1)} %copy-done.4), channel_id=1, source_target_pairs={{0,16},{16,32},{32,48},{48,64},{64,80},{80,96},{96,112},{112,128},... | collective-permute-start | bytes 393224 | tf_op jit(solution)/shard_map/ppermute | solution.py:15
  70.7 29.3 %collective-permute-start.9 = (bf16[128,512]{0,1:T(8,128)(2,1)S(1)}, bf16[128,512]{0,1:T(8,128)(2,1)}, u32[]{:S(2)}, u32[]{:S(2)}) collective-permute-start(bf16[128,512]{0,1:T(8,128)(2,1)S(1)} %fusion.24), channel_id=1, source_target_pairs={{0,16},{16,32},{32,48},{48,64},{64,80},{80,96},{96,112},{112,128},... | collective-permute-start | bytes 393224 | tf_op jit(solution)/shard_map/ppermute | solution.py:15
  72.7 5.3 collective-permute-start
  79.7 24.6 %copy-start.9 = (f32[128,4]{0,1:T(4,128)S(1)}, f32[128,4]{0,1:T(4,128)}, u32[]{:S(2)}) copy-start(f32[128,4]{0,1:T(4,128)} %get-tuple-element.7) | copy-start | bytes 6148
  79.8 19.1 %copy-start.8 = (bf16[640,512]{0,1:T(8,128)(2,1)}, bf16[640,512]{0,1:T(8,128)(2,1)S(1)}, u32[]{:S(2)}) copy-start(bf16[640,512]{0,1:T(8,128)(2,1)S(1)} %constant_dynamic-update-slice_fusion.8) | copy-start | bytes 1966084
  99.2 5.1 copy-start.15
  112.1 0.7 copy-start.11
  112.1 1.3 copy-start.14
  112.1 110.0 %copy-start.3 = (bf16[8,7168]{1,0:T(8,128)(2,1)S(1)}, bf16[8,7168]{1,0:T(8,128)(2,1)}, u32[]{:S(2)}) copy-start(bf16[8,7168]{1,0:T(8,128)(2,1)} %param.19) | copy-start | bytes 344068
  112.1 111.2 %copy-start.7 = (f32[7168]{0:T(1024)S(1)}, f32[7168]{0:T(1024)}, u32[]{:S(2)}) copy-start(f32[7168]{0:T(1024)} %param.20) | copy-start | bytes 86020
  112.1 396.7 %reduce-scatter.2.cloned.1.call-start = ((), (), s32[]{:S(2)}) async-start(), calls=%async_computation.5 | async-start | bytes 7798784 | tf_op jit(solution)/shard_map/reduce_scatter | solution.py:181
  430.5 5.8 %copy-start.1 = (bf16[512,7168]{1,0:T(8,128)(2,1)S(1)}, bf16[512,7168]{1,0:T(8,128)(2,1)}, u32[]{:S(2)}) copy-start(bf16[512,7168]{1,0:T(8,128)(2,1)} %reshape_reshape.3) | copy-start | bytes 22020100
  430.5 6.2 %copy-start.13 = (bf16[1,7168,128]{2,1,0:T(8,128)(2,1)S(1)}, bf16[1,7168,128]{2,1,0:T(8,128)(2,1)}, u32[]{:S(2)}) copy-start(bf16[1,7168,128]{2,1,0:T(8,128)(2,1)} %param.24) | copy-start | bytes 5505028
  443.8 74.6 %copy-start.12 = (f32[8,2]{0,1:T(2,128)S(1)}, f32[8,2]{0,1:T(2,128)}, u32[]{:S(2)}) copy-start(f32[8,2]{0,1:T(2,128)} %param.22) | copy-start | bytes 196
  511.1 15.6 %all-to-all-start.2 = ((bf16[16,2,7168]{2,1,0:T(2,128)(2,1)}), bf16[16,2,7168]{2,1,0:T(2,128)(2,1)S(1)}, u32[]{:S(2)}, u32[]{:S(2)}) async-start(bf16[16,2,7168]{2,1,0:T(2,128)(2,1)} %copy.99), calls=%async_computation.3 | async-start | bytes 917504 | tf_op jit(solution)/shard_map/all_to_all | solution.py:184
Sparse Core Ops, SparseCore 0:
  9.2 68.1 all-gather.1
  112.3 109.8 all-reduce.2
  443.9 64.8 reduce-scatter.1
